TPU v7x, 32 devices: a whole 2x2x4 slice. The times are simulated.
32 devices in a mesh: dp: 16 (over z, x, core), seq: 2 (over y).
Axes of the slice: x: 2, y: 2, z: 4, core: 2. Of those that a mesh axis runs over, the one named last changes fastest.
Arguments:
- tokens: bfloat16 [32, 512, 768], P('dp', 'seq'), may hold values from -6 to 6
- cotangent: bfloat16 [32, 512, 768], P('dp', 'seq'), may hold values from -6 to 6
- lengths: int32 [32], P('dp'), may hold values from 1 to 512, 12288 in all
- query_weight: bfloat16 [768, 768], replicated, may hold values from -0.21875 to 0.21875
- query_bias: float32 [768], replicated, may hold values from -1.2 to 1.2
- key_weight: bfloat16 [768, 768], replicated, may hold values from -0.21875 to 0.21875
- value_weight: bfloat16 [768, 768], replicated, may hold values from -0.21875 to 0.21875
- value_bias: float32 [768], replicated, may hold values from -0.3 to 0.3
- mixer_weight: bfloat16 [768, 768], replicated, may hold values from -3.5 to 3.5
- mixer_bias: float32 [768], replicated, may hold values from -1.2 to 1.2
- first_gain: float32 [768], replicated, may hold values from 0.25 to 1.75
- first_bias: float32 [768], replicated, may hold values from -1.2 to 1.2
- inner_weight: bfloat16 [768, 3072], replicated, may hold values from -0.21875 to 0.21875
- inner_bias: float32 [3072], replicated, may hold values from -1.2 to 1.2
- outer_weight: bfloat16 [3072, 768], replicated, may hold values from -0.109375 to 0.109375
- outer_bias: float32 [768], replicated, may hold values from -1.2 to 1.2
- second_gain: float32 [768], replicated, may hold values from 0.25 to 1.75
- second_bias: float32 [768], replicated, may hold values from -1.2 to 1.2
Outputs:
- layer_output: float32 [32, 512, 768], P('dp', 'seq')
- input_gradient: float32 [32, 512, 768], P('dp', 'seq')
- weight_query: float32 [768, 768], P('dp', 'seq')
- weight_key: float32 [768, 768], P('dp', 'seq')
- weight_value: float32 [768, 768], P('dp', 'seq')
- weight_mixer: float32 [768, 768], P('dp', 'seq')
- weight_inner: float32 [768, 3072], P('dp', 'seq')
- weight_outer: float32 [3072, 768], P('dp', 'seq')
- bias_query: float32 [768], replicated
- bias_value: float32 [768], replicated
- bias_mixer: float32 [768], replicated
- bias_inner: float32 [3072], replicated
- bias_outer: float32 [768], replicated
- gain_first: float32 [768], replicated
- bias_first: float32 [768], replicated
- gain_second: float32 [768], replicated
- bias_second: float32 [768], replicated
Inputs may be any that keep to these rules, and one draw needn't show every extreme that they name: `lengths`: positions from a slot's length to 511 are padding; some slot has exactly 512 tokens.
All inputs are finite; a program needn't handle non-finite values. No bound on the sum of `lengths` on one device may be relied on, other than what follows from the above.
Results may differ from a plain program's by a relative error of at most 0.017.
Values may be sent and summed in bfloat16 or wider, within the bound.
No kernel may reach another device: no remote copies, remote signals or barrier semaphores. Data moves between devices by JAX's collectives and lax.ppermute only.
A program may use at most 192 MiB of HBM per device.

v0:
```python
import math
import jax
import jax.numpy as jnp
from jax import lax
from jax.sharding import PartitionSpec as P

HEADS = 12
gelu_scale = math.sqrt(2.0 / math.pi)


def normalize(residue, gain, shift):
    average = jnp.mean(residue, -1, keepdims=True)
    centred = residue - average
    variance = jnp.mean(centred * centred, -1, keepdims=True)
    return centred * lax.rsqrt(variance + 1e-05) * gain + shift


def smooth(pre_act):
    return (
        0.5
        * pre_act
        * (1.0 + jnp.tanh(gelu_scale * (pre_act + 0.044715 * pre_act * pre_act * pre_act)))
    )


def product(left, right):
    return jnp.dot(left, right, preferred_element_type=jnp.float32)


def across(left, right):
    return lax.dot_general(
        left, right, (((0,), (0,)), ((), ())), preferred_element_type=jnp.float32
    )


def against(left, right):
    return lax.dot_general(
        left, right, (((1,), (1,)), ((), ())), preferred_element_type=jnp.float32
    )


def column_sums(matrix):
    return jnp.sum(matrix.astype(jnp.float32), 0)


def local(
    tokens,
    cotangent,
    lengths,
    query_weight,
    query_bias,
    key_weight,
    value_weight,
    value_bias,
    mixer_weight,
    mixer_bias,
    first_gain,
    first_bias,
    inner_weight,
    inner_bias,
    outer_weight,
    outer_bias,
    second_gain,
    second_bias,
):
    slots, own_length, breadth = tokens.shape
    head_count = HEADS
    head_width = breadth // head_count
    token_rows = tokens.reshape(slots * own_length, breadth)
    queries = (product(token_rows, query_weight) + query_bias).astype(jnp.bfloat16)
    own_keys = (
        product(token_rows, key_weight).astype(jnp.bfloat16).reshape(slots, own_length, breadth)
    )
    own_values = (
        (product(token_rows, value_weight) + value_bias)
        .astype(jnp.bfloat16)
        .reshape(slots, own_length, breadth)
    )
    all_keys, all_values = (
        lax.all_gather(own_keys, "seq", axis=1, tiled=True),
        lax.all_gather(own_values, "seq", axis=1, tiled=True),
    )
    length = all_keys.shape[1]
    usable = jnp.arange(length, dtype=jnp.int32)[None, :] < lengths[:, None]
    query_heads = queries.reshape(slots, own_length, head_count, head_width)
    key_heads = all_keys.reshape(slots, length, head_count, head_width)
    value_heads = all_values.reshape(slots, length, head_count, head_width)

    def scores_of():
        raw_scores = (
            jnp.einsum(
                "sqhd,skhd->shqk", query_heads, key_heads, preferred_element_type=jnp.float32
            )
            * 0.125
        )
        return jnp.where(usable[:, None, None, :], raw_scores, -1000000000.0)

    masked = scores_of()
    row_top = jnp.max(masked, -1, keepdims=True)
    raised = jnp.exp(masked - row_top)
    totals = jnp.sum(raised, -1, keepdims=True)
    logsum = row_top + jnp.log(totals)
    shares_low = (raised / totals).astype(jnp.bfloat16)
    context = jnp.einsum(
        "shqk,skhd->sqhd", shares_low, value_heads, preferred_element_type=jnp.float32
    )
    context = context.reshape(slots * own_length, breadth).astype(jnp.bfloat16)
    mixed = product(context, mixer_weight) + mixer_bias
    normed_one, first_back = jax.vjp(
        normalize, token_rows.astype(jnp.float32) + mixed, first_gain, first_bias
    )
    normed_low = normed_one.astype(jnp.bfloat16)
    inner_pre = product(normed_low, inner_weight) + inner_bias
    active_f, active_back = jax.vjp(smooth, inner_pre)
    active = active_f.astype(jnp.bfloat16)
    outer_out = product(active, outer_weight) + outer_bias
    layer_output, second_back = jax.vjp(normalize, normed_one + outer_out, second_gain, second_bias)
    tangent = cotangent.reshape(slots * own_length, breadth).astype(jnp.float32)
    slope_second, gain_second, bias_second = second_back(tangent)
    second_low = slope_second.astype(jnp.bfloat16)
    weight_outer = across(active, second_low)
    bias_outer = column_sums(second_low)
    (slope_active,) = active_back(against(second_low, outer_weight))
    slope_inner = slope_active.astype(jnp.bfloat16)
    weight_inner = across(normed_low, slope_inner)
    bias_inner = column_sums(slope_inner)
    slope_first = slope_second + against(slope_inner, inner_weight)
    slope_mixed, gain_first, bias_first = first_back(slope_first)
    mixed_low = slope_mixed.astype(jnp.bfloat16)
    weight_mixer = across(context, mixed_low)
    bias_mixer = column_sums(mixed_low)
    slope_context = against(mixed_low, mixer_weight).astype(jnp.bfloat16)
    slope_context = slope_context.reshape(slots, own_length, head_count, head_width)
    shares = jnp.exp(scores_of() - logsum)
    slope_shares = jnp.einsum(
        "sqhd,skhd->shqk", slope_context, value_heads, preferred_element_type=jnp.float32
    )
    row_inner = jnp.sum(slope_shares * shares, -1, keepdims=True)
    slope_scores = (shares * (slope_shares - row_inner)).astype(jnp.bfloat16)
    slope_queries = (
        jnp.einsum("shqk,skhd->sqhd", slope_scores, key_heads, preferred_element_type=jnp.float32)
        * 0.125
    )
    slope_queries = slope_queries.reshape(slots * own_length, breadth).astype(jnp.bfloat16)
    key_terms = (
        jnp.einsum("shqk,sqhd->skhd", slope_scores, query_heads, preferred_element_type=jnp.float32)
        * 0.125
    )
    value_terms = jnp.einsum(
        "shqk,sqhd->skhd",
        shares.astype(jnp.bfloat16),
        slope_context,
        preferred_element_type=jnp.float32,
    )
    key_terms = key_terms.reshape(slots, length, breadth)
    value_terms = value_terms.reshape(slots, length, breadth)
    slope_keys, slope_values = (
        lax.psum_scatter(
            key_terms.astype(jnp.bfloat16), "seq", scatter_dimension=1, tiled=True
        ).astype(jnp.float32),
        lax.psum_scatter(
            value_terms.astype(jnp.bfloat16), "seq", scatter_dimension=1, tiled=True
        ).astype(jnp.float32),
    )
    keys_low = slope_keys.reshape(slots * own_length, breadth).astype(jnp.bfloat16)
    values_low = slope_values.reshape(slots * own_length, breadth).astype(jnp.bfloat16)
    weight_query = across(token_rows, slope_queries)
    bias_query = column_sums(slope_queries)
    weight_key = across(token_rows, keys_low)
    weight_value = across(token_rows, values_low)
    bias_value = column_sums(values_low)
    input_gradient = (
        slope_mixed
        + against(slope_queries, query_weight)
        + against(keys_low, key_weight)
        + against(values_low, value_weight)
    )
    part_query, part_key, part_value, part_mixer, part_inner, part_outer = (
        lax.psum_scatter(
            weight_query.astype(jnp.bfloat16), "seq", scatter_dimension=1, tiled=True
        ).astype(jnp.float32),
        lax.psum_scatter(
            weight_key.astype(jnp.bfloat16), "seq", scatter_dimension=1, tiled=True
        ).astype(jnp.float32),
        lax.psum_scatter(
            weight_value.astype(jnp.bfloat16), "seq", scatter_dimension=1, tiled=True
        ).astype(jnp.float32),
        lax.psum_scatter(
            weight_mixer.astype(jnp.bfloat16), "seq", scatter_dimension=1, tiled=True
        ).astype(jnp.float32),
        lax.psum_scatter(
            weight_inner.astype(jnp.bfloat16), "seq", scatter_dimension=1, tiled=True
        ).astype(jnp.float32),
        lax.psum_scatter(
            weight_outer.astype(jnp.bfloat16), "seq", scatter_dimension=1, tiled=True
        ).astype(jnp.float32),
    )
    summed = (
        lax.psum_scatter(part_query, "dp", scatter_dimension=0, tiled=True),
        lax.psum_scatter(part_key, "dp", scatter_dimension=0, tiled=True),
        lax.psum_scatter(part_value, "dp", scatter_dimension=0, tiled=True),
        lax.psum_scatter(part_mixer, "dp", scatter_dimension=0, tiled=True),
        lax.psum_scatter(part_inner, "dp", scatter_dimension=0, tiled=True),
        lax.psum_scatter(part_outer, "dp", scatter_dimension=0, tiled=True),
    )
    vectors = lax.psum(
        (
            bias_query,
            bias_value,
            bias_mixer,
            bias_inner,
            bias_outer,
            gain_first,
            bias_first,
            gain_second,
            bias_second,
        ),
        ("dp", "seq"),
    )
    return (
        layer_output.reshape(slots, own_length, breadth),
        input_gradient.reshape(slots, own_length, breadth),
        summed[0],
        summed[1],
        summed[2],
        summed[3],
        summed[4],
        summed[5],
        vectors[0],
        vectors[1],
        vectors[2],
        vectors[3],
        vectors[4],
        vectors[5],
        vectors[6],
        vectors[7],
        vectors[8],
    )


def solution(mesh):
    placed = (
        P("dp", "seq", None),
        P("dp", "seq", None),
        P("dp"),
        P(),
        P(),
        P(),
        P(),
        P(),
        P(),
        P(),
        P(),
        P(),
        P(),
        P(),
        P(),
        P(),
        P(),
        P(),
    )
    return jax.shard_map(
        local,
        mesh=mesh,
        in_specs=placed,
        out_specs=(
            P("dp", "seq", None),
            P("dp", "seq", None),
            P("dp", "seq"),
            P("dp", "seq"),
            P("dp", "seq"),
            P("dp", "seq"),
            P("dp", "seq"),
            P("dp", "seq"),
            P(),
            P(),
            P(),
            P(),
            P(),
            P(),
            P(),
            P(),
            P(),
        ),
        check_vma=False,
    )
```

profile of v0, /device:TPU:0, one launch (start us, length us, event | category | flops | bytes accessed | tf_op | source)
XLA Modules:
  0.0 814.7 jit_solution(2650582798111291371)
XLA Ops:
  7.3 3.3 convolution_convert_fusion.5
  12.6 2.0 add_convert_fusion
  15.1 25.6 %all-gather.5.cloned.1.call-done = bf16[2,512,768]{2,1,0:T(8,128)(2,1)} async-done(((bf16[2,256,768]{2,1,0:T(8,128)(2,1)}), bf16[2,512,768]{2,1,0:T(8,128)(2,1)}) %all-gather.5.cloned.1.call-update) | async-done | bytes 1572880 | tf_op jit(solution)/shard_map/all_gather | solution.py:80
  42.4 2.3 fusion.12
  44.7 3.3 fusion
  50.1 19.9 %all-gather.3.cloned.1.call-done = bf16[2,512,768]{2,1,0:T(8,128)(2,1)} async-done(((bf16[2,256,768]{2,1,0:T(8,128)(2,1)}), bf16[2,512,768]{2,1,0:T(8,128)(2,1)}) %all-gather.3.cloned.1.call-update) | async-done | bytes 1572880 | tf_op jit(solution)/shard_map/all_gather | solution.py:81
  71.8 7.5 fusion.25
  82.2 5.7 fusion.40
  87.9 4.2 fusion.46
  96.7 8.2 %convert_reduce_fusion = (f32[3072]{0:T(1024)}, bf16[512,3072]{1,0:T(8,128)(2,1)S(1)}) fusion(f32[512,3072]{1,0:T(8,128)S(1)} %fusion.40, f32[3072]{0:T(1024)S(1)} %copy-done.38, bf16[512,768]{1,0:T(8,128)(2,1)S(1)} %get-tuple-element.83, bf16[3072,768]{1,0:T(8,128)(2,1)S(1)} %bitcast.128), kind=kOutput, calls=%fused_computation.19 | convolution fusion | flops 2458383360 | bytes 14966784 | tf_op jit(solution)/shard_map/dot_general | solution.py:37
  104.9 3.7 multiply_reduce_fusion.1
  112.7 2.3 copy.66
  115.0 2.6 reshape.184
  117.6 7.4 fusion.13
  125.0 2.6 copy.72
  127.7 8.0 multiply_reduce_fusion
  135.8 6.8 multiply_convert_fusion
  142.6 2.7 multiply_convert_fusion.2
  145.7 2.6 copy.70
  149.5 1.9 convolution_convert_fusion.2
  152.9 5.4 convert_reduce_fusion.5
  161.6 3.2 fusion.22
  164.9 17.4 %reduce-scatter.25.cloned.1.call-done = bf16[2,256,768]{2,1,0:T(8,128)(2,1)} async-done(((bf16[2,512,768]{2,1,0:T(8,128)(2,1)}), bf16[2,256,768]{2,1,0:T(8,128)(2,1)}) %reduce-scatter.25.cloned.1.call-update) | async-done | bytes 786448 | tf_op jit(solution)/shard_map/reduce_scatter | solution.py:158
  182.2 3.0 fusion.21
  185.3 7.4 convolution_convert_fusion.1
  193.9 8.7 %convolution_convert_fusion = bf16[3072,768]{1,0:T(8,128)(2,1)} fusion(bf16[512,768]{1,0:T(8,128)(2,1)S(1)} %copy-done.17, f32[512,3072]{1,0:T(8,128)} %copy-done.46, f32[3072]{0:T(1024)S(1)} %copy-done.39), kind=kOutput, calls=%fused_computation.24 | convolution fusion | flops 2434007040 | bytes 11808768 | tf_op jit(solution)/shard_map/dot_general | solution.py:31
  202.6 6.7 copy.88
  211.9 18.8 %reduce-scatter.29.cloned.1.call-done = bf16[768,384]{0,1:T(8,128)(2,1)} async-done(((bf16[768,768]{0,1:T(8,128)(2,1)}), bf16[768,384]{0,1:T(8,128)(2,1)}) %reduce-scatter.29.cloned.1.call-update) | async-done | bytes 589840 | tf_op jit(solution)/shard_map/reduce_scatter | solution.py:179
  230.7 2.4 copy.80
  233.2 21.7 %reduce-scatter.33.cloned.1.call-done = bf16[768,384]{0,1:T(8,128)(2,1)} async-done(((bf16[768,768]{0,1:T(8,128)(2,1)}), bf16[768,384]{0,1:T(8,128)(2,1)}) %reduce-scatter.33.cloned.1.call-update) | async-done | bytes 589840 | tf_op jit(solution)/shard_map/reduce_scatter | solution.py:185
  254.9 2.3 copy.84
  257.3 21.7 %reduce-scatter.31.cloned.1.call-done = bf16[768,384]{0,1:T(8,128)(2,1)} async-done(((bf16[768,768]{0,1:T(8,128)(2,1)}), bf16[768,384]{0,1:T(8,128)(2,1)}) %reduce-scatter.31.cloned.1.call-update) | async-done | bytes 589840 | tf_op jit(solution)/shard_map/reduce_scatter | solution.py:182
  279.0 2.3 copy.82
  281.4 60.0 %reduce-scatter.37.cloned.1.call-done = bf16[768,1536]{1,0:T(8,128)(2,1)} async-done(((bf16[768,3072]{1,0:T(8,128)(2,1)}), bf16[768,1536]{1,0:T(8,128)(2,1)}) %reduce-scatter.37.cloned.1.call-update) | async-done | bytes 2359312 | tf_op jit(solution)/shard_map/reduce_scatter | solution.py:191
  341.4 4.4 convert_element_type.203
  345.9 57.8 %reduce-scatter.51.cloned.1.call-done = bf16[384,3072]{1,0:T(8,128)(2,1)} async-done(((bf16[768,3072]{1,0:T(8,128)(2,1)}), bf16[384,3072]{1,0:T(8,128)(2,1)}) %reduce-scatter.51.cloned.1.call-update) | async-done | bytes 2359312
  403.6 4.3 copy.89
  407.9 4.2 convert_element_type.205
  413.5 3.6 fusion.47
  417.3 41.1 %all-reduce = (f32[768]{0:T(1024)}, f32[768]{0:T(1024)}, f32[768]{0:T(1024)}, f32[3072]{0:T(1024)}, f32[768]{0:T(1024)}, /*index=5*/f32[768]{0:T(1024)}, f32[768]{0:T(1024)}, f32[768]{0:T(1024)}, f32[768]{0:T(1024)}) all-reduce(f32[768]{0:T(1024)S(1)} %reduce_sum.216, ...), channel_id=1, replica_groups=mesh['dp'=16,'seq'=2] {'dp','seq'}, use_global_device_ids=true, to_apply=%region_26.27 | all-reduce | flops 9216 | bytes 73728 | tf_op jit(solution)/shard_map/psum | solution.py:206
  458.4 2.2 fusion.48
  460.7 2.1 add_add_fusion.2
  462.7 3.3 reduce-scatter.35.cloned.1.call-done
  466.1 61.3 %reduce-scatter.43.cloned.1.call-done = f32[48,384]{1,0:T(8,128)} async-done(((f32[768,384]{1,0:T(8,128)}), f32[48,384]{1,0:T(8,128)}) %reduce-scatter.43.cloned.1.call-update) | async-done | bytes 73744
  527.3 61.4 %reduce-scatter.47.cloned.1.call-done = f32[48,384]{1,0:T(8,128)} async-done(((f32[768,384]{1,0:T(8,128)}), f32[48,384]{1,0:T(8,128)}) %reduce-scatter.47.cloned.1.call-update) | async-done | bytes 73744
  588.7 61.2 %reduce-scatter.45.cloned.1.call-done = f32[48,384]{1,0:T(8,128)} async-done(((f32[768,384]{1,0:T(8,128)}), f32[48,384]{1,0:T(8,128)}) %reduce-scatter.45.cloned.1.call-update) | async-done | bytes 73744
  649.9 78.9 %reduce-scatter.39.cloned.1.call-done = f32[48,1536]{1,0:T(8,128)} async-done(((f32[768,1536]{1,0:T(8,128)}), f32[48,1536]{1,0:T(8,128)}) %reduce-scatter.39.cloned.1.call-update) | async-done | bytes 294928 | tf_op jit(solution)/shard_map/reduce_scatter | solution.py:203
  728.8 79.1 %reduce-scatter.41.cloned.1.call-done = f32[192,384]{1,0:T(8,128)} async-done(((f32[3072,384]{1,0:T(8,128)}), f32[192,384]{1,0:T(8,128)}) %reduce-scatter.41.cloned.1.call-update) | async-done | bytes 294928 | tf_op jit(solution)/shard_map/reduce_scatter | solution.py:204
  (175 shorter events, 31.3 us)
Async XLA Ops:
  7.2 73.1 %copy-start = (bf16[768,768]{1,0:T(8,128)(2,1)S(1)}, bf16[768,768]{1,0:T(8,128)(2,1)}, u32[]{:S(2)}) copy-start(bf16[768,768]{1,0:T(8,128)(2,1)} %param.26) | copy-start | bytes 3538948
  7.2 33.5 %all-gather.5.cloned.1.call-start = ((), (), s32[]{:S(2)}) async-start(), calls=%async_computation.15 | async-start | bytes 2359296 | tf_op jit(solution)/shard_map/all_gather | solution.py:80
  7.2 3.5 copy-start.11
  7.3 3.5 copy-start.34
  7.3 3.4 copy-start.40
  10.7 59.4 %all-gather.3.cloned.1.call-start = ((), (), s32[]{:S(2)}) async-start(), calls=%async_computation.14 | async-start | bytes 2359296 | tf_op jit(solution)/shard_map/all_gather | solution.py:81
  12.4 149.1 %reduce-scatter.27.cloned.1.call-start = ((), (), s32[]{:S(2)}) async-start(), calls=%async_computation.17 | async-start | bytes 2359296 | tf_op jit(solution)/shard_map/reduce_scatter | solution.py:161
  42.4 2.3 copy-start.4
  44.7 4.6 copy-start.2
  44.7 4.7 copy-start.19
  71.7 7.5 copy-start.7
  81.4 27.2 %copy-start.8 = (f32[512,768]{1,0:T(8,128)}, f32[512,768]{1,0:T(8,128)S(1)}, u32[]{:S(2)}) copy-start(f32[512,768]{1,0:T(8,128)S(1)} %get-tuple-element.96) | copy-start | bytes 4718596
  81.4 6.5 slice-start
  82.2 26.5 %copy-start.26 = (f32[512]{0:T(512)}, f32[512]{0:T(512)S(1)}, u32[]{:S(2)}) copy-start(f32[512]{0:T(512)S(1)} %fusion.33) | copy-start | bytes 6148
  82.2 5.7 slice-start.1
  82.2 5.7 copy-start.38
  82.2 5.7 copy-start.43
  87.9 8.7 %copy-start.46 = (f32[512,3072]{1,0:T(8,128)}, f32[512,3072]{1,0:T(8,128)S(1)}, u32[]{:S(2)}) copy-start(f32[512,3072]{1,0:T(8,128)S(1)} %fusion.40) | copy-start | bytes 18874372
  95.9 9.0 %slice-start.2 = ((s8[4718592]{0:T(1024)(128)(4,1)}), s8[4194304]{0:T(1024)(128)(4,1)S(1)}, s32[]{:S(2)}) async-start(s8[4718592]{0:T(1024)(128)(4,1)} %bitcast.129), calls=%async_computation.32 | async-start | bytes 8388608
  96.7 8.2 %copy-start.16 = (bf16[512,768]{1,0:T(8,128)(2,1)}, bf16[512,768]{1,0:T(8,128)(2,1)S(1)}, u32[]{:S(2)}) copy-start(bf16[512,768]{1,0:T(8,128)(2,1)S(1)} %get-tuple-element.83) | copy-start | bytes 2359300
  96.7 8.2 %slice-start.3 = ((s8[4718592]{0:T(1024)(128)(4,1)}), s8[524288]{0:T(1024)(128)(4,1)S(1)}, s32[]{:S(2)}) async-start(s8[4718592]{0:T(1024)(128)(4,1)} %bitcast.129), calls=%async_computation.33 | async-start | bytes 1048576
  104.9 3.7 copy-start.47
  112.7 4.9 copy-start.20
  127.7 54.6 %reduce-scatter.25.cloned.1.call-start = ((), (), s32[]{:S(2)}) async-start(), calls=%async_computation.16 | async-start | bytes 2359296 | tf_op jit(solution)/shard_map/reduce_scatter | solution.py:158
  142.6 3.1 copy-start.3
  148.4 61.0 %reduce-scatter.49.cloned.1.call-start = ((), (), s32[]{:S(2)}) async-start(), calls=%async_computation.28 | async-start | bytes 1769472
  152.9 77.9 %reduce-scatter.29.cloned.1.call-start = ((), (), s32[]{:S(2)}) async-start(), calls=%async_computation.18 | async-start | bytes 1769472 | tf_op jit(solution)/shard_map/reduce_scatter | solution.py:179
  161.3 93.5 %reduce-scatter.33.cloned.1.call-start = ((), (), s32[]{:S(2)}) async-start(), calls=%async_computation.20 | async-start | bytes 1769472 | tf_op jit(solution)/shard_map/reduce_scatter | solution.py:185
  164.8 20.5 %copy-start.27 = (f32[512]{0:T(512)S(1)}, f32[512]{0:T(512)}, u32[]{:S(2)}) copy-start(f32[512]{0:T(512)} %copy-done.26) | copy-start | bytes 6148
  164.8 20.5 %copy-start.32 = (f32[768]{0:T(1024)S(1)}, f32[768]{0:T(1024)}, u32[]{:S(2)}) copy-start(f32[768]{0:T(1024)} %param.28) | copy-start | bytes 9220
  164.8 20.5 %copy-start.45 = (f32[768]{0:T(1024)S(1)}, f32[768]{0:T(1024)}, u32[]{:S(2)}) copy-start(f32[768]{0:T(1024)} %param.29) | copy-start | bytes 9220
  164.8 114.2 %reduce-scatter.31.cloned.1.call-start = ((), (), s32[]{:S(2)}) async-start(), calls=%async_computation.19 | async-start | bytes 1769472 | tf_op jit(solution)/shard_map/reduce_scatter | solution.py:182
  185.2 156.2 %reduce-scatter.37.cloned.1.call-start = ((), (), s32[]{:S(2)}) async-start(), calls=%async_computation.22 | async-start | bytes 7077888 | tf_op jit(solution)/shard_map/reduce_scatter | solution.py:191
  192.8 210.8 %reduce-scatter.51.cloned.1.call-start = ((), (), s32[]{:S(2)}) async-start(), calls=%async_computation.29 | async-start | bytes 7077888
  209.3 256.8 %reduce-scatter.35.cloned.1.call-start = ((), (), s32[]{:S(2)}) async-start(), calls=%async_computation.21 | async-start | bytes 1253376 | tf_op jit(solution)/shard_map/reduce_scatter | solution.py:202
  211.9 315.4 %reduce-scatter.43.cloned.1.call-start = ((), (), s32[]{:S(2)}) async-start(), calls=%async_computation.25 | async-start | bytes 1253376
  233.1 355.6 %reduce-scatter.47.cloned.1.call-start = ((), (), s32[]{:S(2)}) async-start(), calls=%async_computation.27 | async-start | bytes 1253376
  257.2 392.7 %reduce-scatter.45.cloned.1.call-start = ((), (), s32[]{:S(2)}) async-start(), calls=%async_computation.26 | async-start | bytes 1253376
  281.3 447.5 %reduce-scatter.39.cloned.1.call-start = ((), (), s32[]{:S(2)}) async-start(), calls=%async_computation.23 | async-start | bytes 5013504 | tf_op jit(solution)/shard_map/reduce_scatter | solution.py:203
  345.8 462.1 %reduce-scatter.41.cloned.1.call-start = ((), (), s32[]{:S(2)}) async-start(), calls=%async_computation.24 | async-start | bytes 5013504 | tf_op jit(solution)/shard_map/reduce_scatter | solution.py:204
  413.4 3.7 copy-start.9
  413.4 3.8 copy-start.22
  413.4 3.8 copy-start.23
  413.4 3.8 copy-start.25
  413.4 3.8 copy-start.28
  413.4 3.8 copy-start.29
  413.4 45.0 %copy-start.37 = (bf16[2,256,768]{2,1,0:T(8,128)(2,1)S(1)}, bf16[2,256,768]{2,1,0:T(8,128)(2,1)}, u32[]{:S(2)}) copy-start(bf16[2,256,768]{2,1,0:T(8,128)(2,1)} %reduce-scatter.25.cloned.1.call-done) | copy-start | bytes 2359300
  460.7 347.3 %copy-start.1 = (bf16[768,768]{1,0:T(8,128)(2,1)S(1)}, bf16[768,768]{1,0:T(8,128)(2,1)}, u32[]{:S(2)}) copy-start(bf16[768,768]{1,0:T(8,128)(2,1)} %param.26) | copy-start | bytes 3538948
  (20 other events, 26.1 us)
Sparse Core Ops, SparseCore 0:
  10.7 29.9 all-gather.4
  42.8 27.1 all-gather.2
  127.8 26.1 reduce-scatter.26
  156.1 26.1 reduce-scatter.24
  184.3 21.8 reduce-scatter.48
  208.9 21.8 reduce-scatter.28
  233.0 21.8 reduce-scatter.32
  257.1 21.8 reduce-scatter.30
  281.3 60.0 reduce-scatter.36
  343.5 60.0 reduce-scatter.50
  407.8 58.2 reduce-scatter.34
  470.1 57.1 reduce-scatter.42
  531.5 57.1 reduce-scatter.46
  592.8 57.1 reduce-scatter.44
  654.2 74.5 reduce-scatter.38
  733.1 74.7 reduce-scatter.40
where the time goes:
time: 824 us; the launch traced here: 815 us
  waiting for transfers between devices  588 us (71%)
  matrix products  98.7 us (12%)
  local copies, waits for them, and re-layouts  44.5 us (5%)
  blocking collectives  41.1 us (5%)
  other arithmetic  26.3 us (3%)
  between operations  14.8 us (2%)
    unnamed x21, waiting for transfers between devices  242 us
    reduce_scatter x1, waiting for transfers between devices, local(): lax.psum_scatter(part_outer, 'dp', scatter_dimension=0, tiled=True)  79.1 us
    reduce_scatter x1, waiting for transfers between devices, local(): lax.psum_scatter(part_inner, 'dp', scatter_dimension=0, tiled=True)  78.9 us
    reduce_scatter x1, waiting for transfers between devices, local(): lax.psum_scatter(weight_inner.astype(jnp.bfloat16), 'seq', scatter_dimens...  60 us
    psum x1, blocking collectives, local(): lax.psum((bias_query, bias_value, bias_mixer, bias_inner, bias_outer, gai...  41.1 us
    unnamed x113, local copies, waits for them, and re-layouts  28.8 us
    dot_general x6, matrix products, across(): lax.dot_general(left, right, (((0,), (0,)), ((), ())), preferred_element_...  26 us
    all_gather x1, waiting for transfers between devices, local(): lax.all_gather(own_keys, 'seq', axis=1, tiled=True)  25.6 us
  transfers between devices with their start and end apart: 16, of which 14 were waited for; matrix products, arithmetic and copies ran while one was open for 13% of the time, Pallas kernels for 0%

commit v1 on v0

--- a/solution.py
+++ b/solution.py
@@ -6,6 +6,14 @@
 
 HEADS = 12
 gelu_scale = math.sqrt(2.0 / math.pi)
+
+
+def gather_by_exchange(shard, axis, dim):
+    count = lax.axis_size(axis)
+    repeats = [count if d == dim else 1 for d in range(shard.ndim)]
+    return lax.all_to_all(
+        jnp.tile(shard, repeats), axis, split_axis=dim, concat_axis=dim, tiled=True
+    )
 
 
 def normalize(residue, gain, shift):
@@ -78,7 +86,7 @@
     )
     all_keys, all_values = (
         lax.all_gather(own_keys, "seq", axis=1, tiled=True),
-        lax.all_gather(own_values, "seq", axis=1, tiled=True),
+        gather_by_exchange(own_values, "seq", 1),
     )
     length = all_keys.shape[1]
     usable = jnp.arange(length, dtype=jnp.int32)[None, :] < lengths[:, None]

time: 824 us -> 815 us (0.989)
  waiting for transfers between devices: 588 us -> 575 us
    all_to_all x0 -> x1, waiting for transfers between devices: none -> 30.2 us  [gather_by_exchange(): lax.all_to_all(jnp.tile(shard, repeats), axis, split_axis=dim, concat_axi...]
    all_gather x1, waiting for transfers between devices: 25.6 us -> 0.01 us  [local(): lax.all_gather(own_keys, 'seq', axis=1, tiled=True)]
    all_gather x1 -> x0, waiting for transfers between devices: 19.9 us -> none  [local(): lax.all_gather(own_values, 'seq', axis=1, tiled=True)]
    unnamed x113 -> x109, local copies, waits for them, and re-layouts: 28.8 us -> 29.3 us
    unnamed x21 -> x20, waiting for transfers between devices: 242 us -> 242 us
  transfers between devices with their start and end apart: 16 -> 16, of which waited for: 14 -> 13; matrix products, arithmetic and copies ran while one was open for 13% -> 13% of each run, Pallas kernels for 0% -> 0%
where the time goes in v1:
time: 815 us; the launch traced here: 807 us
  waiting for transfers between devices  575 us (71%)
  matrix products  92.4 us (11%)
  local copies, waits for them, and re-layouts  52.1 us (6%)
  blocking collectives  41 us (5%)
  other arithmetic  26.3 us (3%)
  between operations  14.8 us (2%)
    unnamed x20, waiting for transfers between devices  242 us
    reduce_scatter x1, waiting for transfers between devices, local(): lax.psum_scatter(part_outer, 'dp', scatter_dimension=0, tiled=True)  79 us
    reduce_scatter x1, waiting for transfers between devices, local(): lax.psum_scatter(part_inner, 'dp', scatter_dimension=0, tiled=True)  78.9 us
    reduce_scatter x1, waiting for transfers between devices, local(): lax.psum_scatter(weight_inner.astype(jnp.bfloat16), 'seq', scatter_dimens...  60 us
    psum x1, blocking collectives, local(): lax.psum((bias_query, bias_value, bias_mixer, bias_inner, bias_outer, gai...  41 us
    all_to_all x1, waiting for transfers between devices, gather_by_exchange(): lax.all_to_all(jnp.tile(shard, repeats), axis, split_axis=dim, concat_axi...  30.2 us
    unnamed x109, local copies, waits for them, and re-layouts  29.3 us
    dot_general x6, matrix products, across(): lax.dot_general(left, right, (((0,), (0,)), ((), ())), preferred_element_...  25.8 us
  transfers between devices with their start and end apart: 16, of which 13 were waited for; matrix products, arithmetic and copies ran while one was open for 13% of the time, Pallas kernels for 0%

profile of v1, /device:TPU:0, one launch (start us, length us, event | category | flops | bytes accessed | tf_op | source)
XLA Modules:
  0.0 806.9 jit_solution(5715957091821173880)
XLA Ops:
  7.3 3.3 convolution_convert_fusion.5
  14.2 4.4 all-to-all-start
  18.6 2.4 add_convert_fusion
  22.2 2.2 reshape.180
  24.6 30.2 %all-to-all-done = bf16[2,512,768]{2,0,1:T(2,128)(2,1)S(1)} async-done(((bf16[2,512,768]{2,0,1:T(2,128)(2,1)}), bf16[2,512,768]{2,0,1:T(2,128)(2,1)S(1)}, u32[]{:S(2)}, u32[]{:S(2)}) %all-to-all-start) | async-done | bytes 1572896 | tf_op jit(solution)/shard_map/all_to_all | solution.py:14
  54.7 3.5 copy.62
  60.0 2.3 fusion.12
  62.3 3.2 fusion
  66.2 2.4 copy-done.2
  68.6 4.9 fusion.25
  76.4 2.7 fusion.40
  79.2 4.2 fusion.46
  87.9 8.2 %convert_reduce_fusion = (f32[3072]{0:T(1024)}, bf16[512,3072]{1,0:T(8,128)(2,1)S(1)}) fusion(f32[512,3072]{1,0:T(8,128)S(1)} %fusion.40, f32[3072]{0:T(1024)S(1)} %copy-done.36, bf16[512,768]{1,0:T(8,128)(2,1)S(1)} %get-tuple-element.83, bf16[3072,768]{1,0:T(8,128)(2,1)S(1)} %bitcast.130), kind=kOutput, calls=%fused_computation.19 | convolution fusion | flops 2458383360 | bytes 14966784 | tf_op jit(solution)/shard_map/dot_general | solution.py:45
  96.1 3.7 multiply_reduce_fusion.1
  103.9 2.3 copy.67
  108.5 7.4 fusion.13
  115.8 2.6 copy.73
  118.5 8.0 multiply_reduce_fusion
  126.6 6.8 multiply_convert_fusion
  133.4 2.7 multiply_convert_fusion.2
  136.6 2.6 copy.71
  143.8 5.4 convert_reduce_fusion.5
  152.2 3.0 fusion.22
  155.3 19.2 %reduce-scatter.25.cloned.1.call-done = bf16[2,256,768]{2,1,0:T(8,128)(2,1)} async-done(((bf16[2,512,768]{2,1,0:T(8,128)(2,1)}), bf16[2,256,768]{2,1,0:T(8,128)(2,1)}) %reduce-scatter.25.cloned.1.call-update) | async-done | bytes 786448 | tf_op jit(solution)/shard_map/reduce_scatter | solution.py:166
  174.5 3.0 fusion.21
  177.6 7.4 convolution_convert_fusion.1
  186.2 8.7 %convolution_convert_fusion = bf16[3072,768]{1,0:T(8,128)(2,1)} fusion(bf16[512,768]{1,0:T(8,128)(2,1)S(1)} %copy-done.17, f32[512,3072]{1,0:T(8,128)} %copy-done.44, f32[3072]{0:T(1024)S(1)} %copy-done.37), kind=kOutput, calls=%fused_computation.24 | convolution fusion | flops 2434007040 | bytes 11808768 | tf_op jit(solution)/shard_map/dot_general | solution.py:39
  194.9 6.7 copy.89
  204.4 18.6 %reduce-scatter.29.cloned.1.call-done = bf16[768,384]{0,1:T(8,128)(2,1)} async-done(((bf16[768,768]{0,1:T(8,128)(2,1)}), bf16[768,384]{0,1:T(8,128)(2,1)}) %reduce-scatter.29.cloned.1.call-update) | async-done | bytes 589840 | tf_op jit(solution)/shard_map/reduce_scatter | solution.py:187
  223.0 2.4 copy.81
  225.4 21.5 %reduce-scatter.33.cloned.1.call-done = bf16[768,384]{0,1:T(8,128)(2,1)} async-done(((bf16[768,768]{0,1:T(8,128)(2,1)}), bf16[768,384]{0,1:T(8,128)(2,1)}) %reduce-scatter.33.cloned.1.call-update) | async-done | bytes 589840 | tf_op jit(solution)/shard_map/reduce_scatter | solution.py:193
  247.0 2.3 copy.85
  249.4 21.7 %reduce-scatter.31.cloned.1.call-done = bf16[768,384]{0,1:T(8,128)(2,1)} async-done(((bf16[768,768]{0,1:T(8,128)(2,1)}), bf16[768,384]{0,1:T(8,128)(2,1)}) %reduce-scatter.31.cloned.1.call-update) | async-done | bytes 589840 | tf_op jit(solution)/shard_map/reduce_scatter | solution.py:190
  271.1 2.3 copy.83
  273.5 60.0 %reduce-scatter.37.cloned.1.call-done = bf16[768,1536]{1,0:T(8,128)(2,1)} async-done(((bf16[768,3072]{1,0:T(8,128)(2,1)}), bf16[768,1536]{1,0:T(8,128)(2,1)}) %reduce-scatter.37.cloned.1.call-update) | async-done | bytes 2359312 | tf_op jit(solution)/shard_map/reduce_scatter | solution.py:199
  333.5 4.4 convert_element_type.203
  338.0 57.9 %reduce-scatter.51.cloned.1.call-done = bf16[384,3072]{1,0:T(8,128)(2,1)} async-done(((bf16[768,3072]{1,0:T(8,128)(2,1)}), bf16[384,3072]{1,0:T(8,128)(2,1)}) %reduce-scatter.51.cloned.1.call-update) | async-done | bytes 2359312
  395.9 4.3 copy.90
  400.2 4.2 convert_element_type.205
  405.8 3.6 fusion.47
  409.6 41.0 %all-reduce = (f32[768]{0:T(1024)}, f32[768]{0:T(1024)}, f32[768]{0:T(1024)}, f32[3072]{0:T(1024)}, f32[768]{0:T(1024)}, /*index=5*/f32[768]{0:T(1024)}, f32[768]{0:T(1024)}, f32[768]{0:T(1024)}, f32[768]{0:T(1024)}) all-reduce(f32[768]{0:T(1024)S(1)} %reduce_sum.216, ...), channel_id=1, replica_groups=mesh['dp'=16,'seq'=2] {'dp','seq'}, use_global_device_ids=true, to_apply=%region_26.27 | all-reduce | flops 9216 | bytes 73728 | tf_op jit(solution)/shard_map/psum | solution.py:214
  450.7 2.2 fusion.48
  455.0 3.2 reduce-scatter.35.cloned.1.call-done
  458.2 61.4 %reduce-scatter.43.cloned.1.call-done = f32[48,384]{1,0:T(8,128)} async-done(((f32[768,384]{1,0:T(8,128)}), f32[48,384]{1,0:T(8,128)}) %reduce-scatter.43.cloned.1.call-update) | async-done | bytes 73744
  519.5 61.3 %reduce-scatter.47.cloned.1.call-done = f32[48,384]{1,0:T(8,128)} async-done(((f32[768,384]{1,0:T(8,128)}), f32[48,384]{1,0:T(8,128)}) %reduce-scatter.47.cloned.1.call-update) | async-done | bytes 73744
  580.8 61.4 %reduce-scatter.45.cloned.1.call-done = f32[48,384]{1,0:T(8,128)} async-done(((f32[768,384]{1,0:T(8,128)}), f32[48,384]{1,0:T(8,128)}) %reduce-scatter.45.cloned.1.call-update) | async-done | bytes 73744
  642.2 78.9 %reduce-scatter.39.cloned.1.call-done = f32[48,1536]{1,0:T(8,128)} async-done(((f32[768,1536]{1,0:T(8,128)}), f32[48,1536]{1,0:T(8,128)}) %reduce-scatter.39.cloned.1.call-update) | async-done | bytes 294928 | tf_op jit(solution)/shard_map/reduce_scatter | solution.py:211
  721.1 79.0 %reduce-scatter.41.cloned.1.call-done = f32[192,384]{1,0:T(8,128)} async-done(((f32[3072,384]{1,0:T(8,128)}), f32[192,384]{1,0:T(8,128)}) %reduce-scatter.41.cloned.1.call-update) | async-done | bytes 294928 | tf_op jit(solution)/shard_map/reduce_scatter | solution.py:212
  (172 shorter events, 36.7 us)
Async XLA Ops:
  7.2 67.3 %copy-start = (bf16[768,768]{1,0:T(8,128)(2,1)S(1)}, bf16[768,768]{1,0:T(8,128)(2,1)}, u32[]{:S(2)}) copy-start(bf16[768,768]{1,0:T(8,128)(2,1)} %param.26) | copy-start | bytes 3538948
  7.2 51.1 %all-gather.2.cloned.1.call-start = ((), (), s32[]{:S(2)}) async-start(), calls=%async_computation.15 | async-start | bytes 2359296 | tf_op jit(solution)/shard_map/all_gather | solution.py:88
  7.2 3.4 copy-start.11
  7.3 3.4 copy-start.32
  7.3 3.4 copy-start.38
  14.2 4.4 copy-start.39
  14.2 40.5 %all-to-all-start = ((bf16[2,512,768]{2,0,1:T(2,128)(2,1)}), bf16[2,512,768]{2,0,1:T(2,128)(2,1)S(1)}, u32[]{:S(2)}, u32[]{:S(2)}) async-start(bf16[2,512,768]{2,0,1:T(2,128)(2,1)} %bitcast.112), calls=%async_computation | async-start | bytes 3145728 | tf_op jit(solution)/shard_map/all_to_all | solution.py:14
  18.6 133.6 %reduce-scatter.27.cloned.1.call-start = ((), (), s32[]{:S(2)}) async-start(), calls=%async_computation.17 | async-start | bytes 2359296 | tf_op jit(solution)/shard_map/reduce_scatter | solution.py:169
  21.1 3.4 copy-start.31
  62.3 6.3 copy-start.2
  62.3 6.3 copy-start.7
  62.3 13.7 %slice-start.2 = ((s8[4718592]{0:T(1024)(128)(4,1)}), s8[4194304]{0:T(1024)(128)(4,1)S(1)}, s32[]{:S(2)}) async-start(s8[4718592]{0:T(1024)(128)(4,1)} %bitcast.131), calls=%async_computation.32 | async-start | bytes 8388608
  68.6 7.4 slice-start.3
  75.6 24.2 %copy-start.8 = (f32[512,768]{1,0:T(8,128)}, f32[512,768]{1,0:T(8,128)S(1)}, u32[]{:S(2)}) copy-start(f32[512,768]{1,0:T(8,128)S(1)} %get-tuple-element.96) | copy-start | bytes 4718596
  75.6 3.5 slice-start
  76.4 23.5 %copy-start.24 = (f32[512]{0:T(512)}, f32[512]{0:T(512)S(1)}, u32[]{:S(2)}) copy-start(f32[512]{0:T(512)S(1)} %fusion.33) | copy-start | bytes 6148
  76.4 2.8 slice-start.1
  76.4 2.8 copy-start.36
  76.4 2.8 copy-start.41
  79.2 8.7 %copy-start.44 = (f32[512,3072]{1,0:T(8,128)}, f32[512,3072]{1,0:T(8,128)S(1)}, u32[]{:S(2)}) copy-start(f32[512,3072]{1,0:T(8,128)S(1)} %fusion.40) | copy-start | bytes 18874372
  87.9 8.2 %copy-start.16 = (bf16[512,768]{1,0:T(8,128)(2,1)}, bf16[512,768]{1,0:T(8,128)(2,1)S(1)}, u32[]{:S(2)}) copy-start(bf16[512,768]{1,0:T(8,128)(2,1)S(1)} %get-tuple-element.83) | copy-start | bytes 2359300
  96.1 3.7 copy-start.45
  103.9 4.6 copy-start.19
  118.5 56.0 %reduce-scatter.25.cloned.1.call-start = ((), (), s32[]{:S(2)}) async-start(), calls=%async_computation.16 | async-start | bytes 2359296 | tf_op jit(solution)/shard_map/reduce_scatter | solution.py:166
  133.4 3.1 copy-start.3
  139.2 62.6 %reduce-scatter.49.cloned.1.call-start = ((), (), s32[]{:S(2)}) async-start(), calls=%async_computation.28 | async-start | bytes 1769472
  143.7 79.3 %reduce-scatter.29.cloned.1.call-start = ((), (), s32[]{:S(2)}) async-start(), calls=%async_computation.18 | async-start | bytes 1769472 | tf_op jit(solution)/shard_map/reduce_scatter | solution.py:187
  152.1 94.8 %reduce-scatter.33.cloned.1.call-start = ((), (), s32[]{:S(2)}) async-start(), calls=%async_computation.20 | async-start | bytes 1769472 | tf_op jit(solution)/shard_map/reduce_scatter | solution.py:193
  155.2 22.3 %copy-start.25 = (f32[512]{0:T(512)S(1)}, f32[512]{0:T(512)}, u32[]{:S(2)}) copy-start(f32[512]{0:T(512)} %copy-done.24) | copy-start | bytes 6148
  155.3 22.3 %copy-start.30 = (f32[768]{0:T(1024)S(1)}, f32[768]{0:T(1024)}, u32[]{:S(2)}) copy-start(f32[768]{0:T(1024)} %param.28) | copy-start | bytes 9220
  155.3 22.3 %copy-start.43 = (f32[768]{0:T(1024)S(1)}, f32[768]{0:T(1024)}, u32[]{:S(2)}) copy-start(f32[768]{0:T(1024)} %param.29) | copy-start | bytes 9220
  155.3 115.8 %reduce-scatter.31.cloned.1.call-start = ((), (), s32[]{:S(2)}) async-start(), calls=%async_computation.19 | async-start | bytes 1769472 | tf_op jit(solution)/shard_map/reduce_scatter | solution.py:190
  177.5 156.0 %reduce-scatter.37.cloned.1.call-start = ((), (), s32[]{:S(2)}) async-start(), calls=%async_computation.22 | async-start | bytes 7077888 | tf_op jit(solution)/shard_map/reduce_scatter | solution.py:199
  185.0 210.9 %reduce-scatter.51.cloned.1.call-start = ((), (), s32[]{:S(2)}) async-start(), calls=%async_computation.29 | async-start | bytes 7077888
  201.5 256.6 %reduce-scatter.35.cloned.1.call-start = ((), (), s32[]{:S(2)}) async-start(), calls=%async_computation.21 | async-start | bytes 1253376 | tf_op jit(solution)/shard_map/reduce_scatter | solution.py:210
  204.3 315.2 %reduce-scatter.43.cloned.1.call-start = ((), (), s32[]{:S(2)}) async-start(), calls=%async_computation.25 | async-start | bytes 1253376
  225.4 355.4 %reduce-scatter.47.cloned.1.call-start = ((), (), s32[]{:S(2)}) async-start(), calls=%async_computation.27 | async-start | bytes 1253376
  249.3 392.9 %reduce-scatter.45.cloned.1.call-start = ((), (), s32[]{:S(2)}) async-start(), calls=%async_computation.26 | async-start | bytes 1253376
  273.5 447.6 %reduce-scatter.39.cloned.1.call-start = ((), (), s32[]{:S(2)}) async-start(), calls=%async_computation.23 | async-start | bytes 5013504 | tf_op jit(solution)/shard_map/reduce_scatter | solution.py:211
  338.0 462.2 %reduce-scatter.41.cloned.1.call-start = ((), (), s32[]{:S(2)}) async-start(), calls=%async_computation.24 | async-start | bytes 5013504 | tf_op jit(solution)/shard_map/reduce_scatter | solution.py:212
  405.8 3.7 copy-start.9
  405.8 3.8 copy-start.20
  405.8 3.8 copy-start.21
  405.8 3.8 copy-start.23
  405.8 3.8 copy-start.26
  405.8 3.8 copy-start.27
  405.8 44.8 %copy-start.35 = (bf16[2,256,768]{2,1,0:T(8,128)(2,1)S(1)}, bf16[2,256,768]{2,1,0:T(8,128)(2,1)}, u32[]{:S(2)}) copy-start(bf16[2,256,768]{2,1,0:T(8,128)(2,1)} %reduce-scatter.25.cloned.1.call-done) | copy-start | bytes 2359300
  452.9 347.2 %copy-start.1 = (bf16[768,768]{1,0:T(8,128)(2,1)S(1)}, bf16[768,768]{1,0:T(8,128)(2,1)}, u32[]{:S(2)}) copy-start(bf16[768,768]{1,0:T(8,128)(2,1)} %param.26) | copy-start | bytes 3538948
  (18 other events, 24.0 us)
Sparse Core Ops, SparseCore 0:
  10.7 45.0 all-gather.1
  118.6 27.4 reduce-scatter.26
  148.3 26.1 reduce-scatter.24
  176.6 21.8 reduce-scatter.48
  201.1 21.8 reduce-scatter.28
  225.1 21.8 reduce-scatter.32
  249.2 21.8 reduce-scatter.30
  273.4 60.0 reduce-scatter.36
  335.8 60.0 reduce-scatter.50
  400.0 58.1 reduce-scatter.34
  462.4 57.1 reduce-scatter.42
  523.6 57.1 reduce-scatter.46
  585.0 57.1 reduce-scatter.44
  646.5 74.5 reduce-scatter.38
  725.4 74.7 reduce-scatter.40
